TPU v7x, 256 devices: a whole 4x4x8 slice. The times are simulated.
256 devices in a mesh: fact: 64 (over z, y, core), feat: 4 (over x).
Axes of the slice: x: 4, y: 4, z: 8, core: 2. Of those that a mesh axis runs over, the one named last changes fastest.
Arguments:
- fact_x: bfloat16 [65536, 512], P('fact', 'feat'), may hold values from -16 to 16
- dim_owner: int32 [65536, 1], P('fact'), may hold values from 0 to 63; in each aligned block of 1024 rows (0 to 1023, 1024 to 2047, ...) at most 48 rows name the same one
- dim_slot: int32 [65536], P('fact'), may hold values from 0 to 127
- fact_owner: int32 [65536, 1], P('fact'), may hold values from 0 to 63; in each aligned block of 1024 rows (0 to 1023, 1024 to 2047, ...) at most 48 rows name the same one
- fact_slot: int32 [65536], P('fact'), may hold values from 0 to 127
- dim_table: bfloat16 [8192, 512], P('fact', 'feat'), may hold values from -6 to 6
- entity_h: bfloat16 [8192, 512], P('fact', 'feat'), may hold values from -16 to 16
- w_msg: bfloat16 [512, 512], P(None, 'feat'), may hold values from -0.25 to 0.25
- w_self: bfloat16 [512, 512], P(None, 'feat'), may hold values from -0.25 to 0.25
- w_neigh: bfloat16 [512, 512], P(None, 'feat'), may hold values from -0.25 to 0.25
- cotangent: bfloat16 [8192, 512], P('fact', 'feat'), may hold values from -0.59765625 to 0.59765625
Outputs:
- output_h: bfloat16 [8192, 512], P('fact', 'feat')
- grad_w_msg: float32 [512, 512], P('fact', 'feat')
- grad_w_self: float32 [512, 512], P('fact', 'feat')
- grad_w_neigh: float32 [512, 512], P('fact', 'feat')
- grad_dim: float32 [8192, 512], P('fact', 'feat')
Inputs may be any that keep to these rules, and one draw needn't show every extreme that they name: `fact_owner`: among the fact rows of one index of fact, no key range is named by more than 48 rows, and some key range by exactly 48. `dim_owner`: among the fact rows of one index of fact, no block of the dimension table is named by more than 48 rows, and some block by exactly 48.
All inputs are finite; a program needn't handle non-finite values.
Results may differ from a plain program's by a relative error of at most 0.0059.
Values may be sent and summed in bfloat16 or wider, within the bound.
A program may use at most 64 MiB of HBM per device.

v0:
```python
import math
import jax
import jax.numpy as jnp
from jax import lax
from jax.sharding import PartitionSpec as P


def silu_slope(values):
    sigmoid_v = jax.nn.sigmoid(values)
    return sigmoid_v * (1.0 + values * (1.0 - sigmoid_v))


def pick_rows(row_keys, table):
    table_rows = table.shape[0]
    block_len = math.gcd(table_rows, 1024)
    num_blocks = table_rows // block_len
    blocks = table.reshape(num_blocks, block_len, table.shape[1])
    columns = lax.iota(jnp.int32, block_len)

    def advance(running, block_no):
        block = lax.dynamic_index_in_dim(blocks, block_no, 0, keepdims=False)
        selector = (row_keys[:, None] == block_no * block_len + columns[None, :]).astype(
            jnp.bfloat16
        )
        return (running + jnp.dot(selector, block, preferred_element_type=jnp.float32), None)

    initial = jnp.zeros((row_keys.shape[0], table.shape[1]), jnp.float32)
    running, _ = lax.scan(advance, initial, jnp.arange(num_blocks, dtype=jnp.int32))
    return running


def sum_rows(row_keys, values, extent):
    block_len = math.gcd(extent, 1024)
    num_blocks = extent // block_len
    targets = lax.iota(jnp.int32, block_len)

    def column_block(block_no):
        selector = (row_keys[None, :] - block_no * block_len == targets[:, None]).astype(
            jnp.bfloat16
        )
        return jnp.dot(selector, values, preferred_element_type=jnp.float32)

    stacked = lax.map(column_block, jnp.arange(num_blocks, dtype=jnp.int32))
    return stacked.reshape(extent, values.shape[1])


def shards(
    fact_x,
    dim_owner,
    dim_slot,
    fact_owner,
    fact_slot,
    dim_table,
    entity_h,
    w_msg,
    w_self,
    w_neigh,
    cotangent,
):
    ent_rows = entity_h.shape[0]
    dim_local = dim_table.shape[0]
    owners = lax.axis_size("fact")
    owner_ids = fact_owner[:, 0]
    entity = owner_ids * ent_rows + fact_slot
    dim_blocks = dim_owner[:, 0]
    fact_dim = dim_blocks * dim_local + dim_slot
    x_full = lax.all_gather(fact_x, "feat", axis=1, tiled=True)
    looked = pick_rows(fact_dim, lax.all_gather(dim_table, "fact", axis=0, tiled=True))
    msg_pre = jnp.dot(x_full, w_msg, preferred_element_type=jnp.float32) + looked
    message = jax.nn.silu(msg_pre).astype(jnp.bfloat16)
    entity_sums = lax.psum_scatter(
        sum_rows(entity, message, ent_rows * lax.axis_size("fact")),
        "fact",
        scatter_dimension=0,
        tiled=True,
    )
    hits = jnp.zeros((ent_rows * owners,), jnp.float32).at[entity].add(1.0)
    counts = lax.psum_scatter(hits, "fact", scatter_dimension=0, tiled=True)
    divisor = jnp.maximum(counts, 1.0)
    aggregate = (entity_sums / divisor[:, None]).astype(jnp.bfloat16)
    h_full, agg_full = (
        lax.all_gather(entity_h, "feat", axis=1, tiled=True),
        lax.all_gather(aggregate, "feat", axis=1, tiled=True),
    )
    pre_act = jnp.dot(h_full, w_self, preferred_element_type=jnp.float32) + jnp.dot(
        agg_full, w_neigh, preferred_element_type=jnp.float32
    )
    output_h = jax.nn.silu(pre_act).astype(jnp.bfloat16)
    d_pre = (cotangent.astype(jnp.float32) * silu_slope(pre_act)).astype(jnp.bfloat16)
    agg_term = jnp.einsum("ej,aj->ea", d_pre, w_neigh, preferred_element_type=jnp.float32)
    d_agg = lax.psum_scatter(agg_term, "feat", scatter_dimension=1, tiled=True)
    d_scaled = (d_agg / divisor[:, None]).astype(jnp.bfloat16)
    d_message = pick_rows(entity, lax.all_gather(d_scaled, "fact", axis=0, tiled=True)).astype(
        jnp.bfloat16
    )
    d_msgpre = (d_message.astype(jnp.float32) * silu_slope(msg_pre)).astype(jnp.bfloat16)
    grad_dim = lax.psum_scatter(
        sum_rows(fact_dim, d_msgpre, dim_local * lax.axis_size("fact")),
        "fact",
        scatter_dimension=0,
        tiled=True,
    )
    self_part = jnp.einsum("ea,eb->ab", h_full, d_pre, preferred_element_type=jnp.float32)
    neigh_part = jnp.einsum("ea,eb->ab", agg_full, d_pre, preferred_element_type=jnp.float32)
    msg_part = jnp.einsum("fa,fb->ab", x_full, d_msgpre, preferred_element_type=jnp.float32)
    grad_w_self, grad_w_neigh, grad_w_msg = (
        lax.psum_scatter(self_part, "fact", scatter_dimension=0, tiled=True),
        lax.psum_scatter(neigh_part, "fact", scatter_dimension=0, tiled=True),
        lax.psum_scatter(msg_part, "fact", scatter_dimension=0, tiled=True),
    )
    return (output_h, grad_w_msg, grad_w_self, grad_w_neigh, grad_dim)


def solution(mesh):
    placed = (
        P("fact", "feat"),
        P("fact", None),
        P("fact"),
        P("fact", None),
        P("fact"),
        P("fact", "feat"),
        P("fact", "feat"),
        P(None, "feat"),
        P(None, "feat"),
        P(None, "feat"),
        P("fact", "feat"),
    )
    return jax.shard_map(
        shards,
        mesh=mesh,
        in_specs=placed,
        out_specs=(
            P("fact", "feat"),
            P("fact", "feat"),
            P("fact", "feat"),
            P("fact", "feat"),
            P("fact", "feat"),
        ),
        check_vma=False,
    )
```

profile of v0, /device:TPU:2, one launch (start us, length us, event | category | flops | bytes accessed | tf_op | source)
XLA Modules:
  0.0 919.5 jit_solution(5410309900059285577)
XLA Ops:
  11.5 79.6 %all-gather.6.cloned.1.call-done = bf16[8192,128]{1,0:T(8,128)(2,1)} async-done(((bf16[128,128]{1,0:T(8,128)(2,1)}), bf16[8192,128]{1,0:T(8,128)(2,1)}) %all-gather.6.cloned.1.call-update) | async-done | bytes 2097168 | tf_op jit(solution)/shard_map/all_gather | solution.py:68
  91.1 40.7 %while.46 = (s32[]{:T(128)}, f32[1024,128]{1,0:T(8,128)S(1)}, s32[1024]{0:T(1024)S(1)}, s32[8]{0:T(128)S(1)}, bf16[8,1024,128]{2,1,0:T(8,128)(2,1)}, /*index=5*/s32[]{:T(128)}, s32[]{:T(128)}, s32[]{:T(128)}, s32[]{:T(128)}) while((s32[]{:T(128)}, f32[1024,128]{1,0:T(8,128)S(1)}, s32[1024]{0:T(1024)S(1)}, s32[8]{0:T(128)S(1)}, ...), condition=%wide.region_1.2_spmd.clone, body=%wide.region_0.1_spmd.clone.sunk | while | flops 269747200 | bytes 1323177 | solution.py:28
  99.3 1.9 fusion.73
  109.5 1.9 fusion.73
  114.6 1.9 fusion.73
  133.5 2.3 broadcast.43.clone
  135.8 22.6 %while.44 = (s32[]{:T(128)}, f32[8,1024,128]{2,1,0:T(8,128)}, s32[8]{0:T(128)S(1)}, s32[1024]{0:T(1024)S(1)}, bf16[1024,128]{1,0:T(8,128)(2,1)S(1)}, /*index=5*/s32[]{:T(128)}, s32[1]{0:T(128)}) while((s32[]{:T(128)}, f32[8,1024,128]{2,1,0:T(8,128)}, s32[8]{0:T(128)S(1)}, s32[1024]{0:T(1024)S(1)}, bf16[1024,128]{1,0:T(8,128)(2,1)S(1)}, ...), condition=%wide.region_3.4_spmd.clone, body=%wide.region_2.3_spmd.clone.sunk | while | flops 269485056 | bytes 799337 | solution.py:43
  160.4 5.9 scatter_custom_fusion
  166.3 248.9 %all-reduce = f32[8192]{0:T(1024)S(1)} all-reduce(f32[8192]{0:T(1024)S(1)} %scatter_custom_fusion), channel_id=3, replica_groups=mesh['fact'=64,'feat'=4] {'fact'}, use_global_device_ids=true, to_apply=%region_6.7.clone | all-reduce | flops 8192 | bytes 65536
  415.2 11.3 %all_gather.15 = bf16[128,512]{1,0:T(8,128)(2,1)S(1)} all-gather(bf16[128,128]{1,0:T(8,128)(2,1)S(1)} %copy-done.4), channel_id=1, replica_groups=mesh['fact'=64,'feat'=4] {'feat'}, dimensions={1}, use_global_device_ids=true | all-gather | bytes 163840 | tf_op jit(solution)/shard_map/all_gather | solution.py:82
  427.7 10.4 %all_gather.18 = bf16[128,512]{1,0:T(8,128)(2,1)S(1)} all-gather(bf16[128,128]{1,0:T(8,128)(2,1)S(1)} %divide_convert_fusion.1), channel_id=1, replica_groups=mesh['fact'=64,'feat'=4] {'feat'}, dimensions={1}, use_global_device_ids=true | all-gather | bytes 163840 | tf_op jit(solution)/shard_map/all_gather | solution.py:83
  439.9 18.9 %reduce-scatter.8.cloned.1.call-done = f32[128,128]{1,0:T(8,128)} async-done(((f32[128,512]{1,0:T(8,128)}), f32[128,128]{1,0:T(8,128)}) %reduce-scatter.8.cloned.1.call-update) | async-done | bytes 65552 | tf_op jit(solution)/shard_map/reduce_scatter | solution.py:91
  462.3 78.6 %all-gather.8.cloned.1.call-done = bf16[8192,128]{1,0:T(8,128)(2,1)} async-done(((bf16[128,128]{1,0:T(8,128)(2,1)}), bf16[8192,128]{1,0:T(8,128)(2,1)}) %all-gather.8.cloned.1.call-update) | async-done | bytes 2097168 | tf_op jit(solution)/shard_map/all_gather | solution.py:93
  540.9 40.7 %while.47 = (s32[]{:T(128)}, f32[1024,128]{1,0:T(8,128)S(1)}, s32[1024]{0:T(1024)S(1)}, s32[8]{0:T(128)S(1)}, bf16[8,1024,128]{2,1,0:T(8,128)(2,1)}, /*index=5*/s32[]{:T(128)}, s32[]{:T(128)}, s32[]{:T(128)}, s32[]{:T(128)}) while((s32[]{:T(128)}, f32[1024,128]{1,0:T(8,128)S(1)}, s32[1024]{0:T(1024)S(1)}, s32[8]{0:T(128)S(1)}, ...), condition=%wide.region_9.10_spmd.clone, body=%wide.region_8.9_spmd.clone.sunk | while | flops 269747200 | bytes 1323177 | solution.py:28
  544.1 1.9 fusion.76
  549.2 1.9 fusion.76
  554.3 1.9 fusion.76
  564.5 1.9 fusion.76
  569.5 1.9 fusion.76
  574.6 1.9 fusion.76
  583.0 2.3 broadcast.43
  585.2 22.6 %while.45 = (s32[]{:T(128)}, f32[8,1024,128]{2,1,0:T(8,128)}, s32[8]{0:T(128)S(1)}, s32[1024]{0:T(1024)S(1)}, bf16[1024,128]{1,0:T(8,128)(2,1)S(1)}, /*index=5*/s32[]{:T(128)}, s32[1]{0:T(128)}) while((s32[]{:T(128)}, f32[8,1024,128]{2,1,0:T(8,128)}, s32[8]{0:T(128)S(1)}, s32[1024]{0:T(1024)S(1)}, ...), condition=%wide.region_14.15_spmd.clone, body=%wide.region_13.14_spmd.clone.sunk | while | flops 269485056 | bytes 799337 | solution.py:43
  608.6 156.2 %all-reduce.7.cloned.1.call-done = (f32[512,128]{0,1:T(8,128)}, f32[512,128]{0,1:T(8,128)}, f32[512,128]{1,0:T(8,128)}) async-done(((f32[512,128]{0,1:T(8,128)}, f32[512,128]{0,1:T(8,128)}, f32[512,128]{1,0:T(8,128)}), (f32[512,128]{0,1:T(8,128)}, f32[512,128]{0,1:T(8,128)}, f32[512,128]{1,0:T(8,128)})) %all-reduce.7.cloned.1.call-update) | async-done | bytes 786448
  768.3 144.4 %reduce-scatter.10.cloned.1.call-done = f32[128,128]{1,0:T(8,128)} async-done(((f32[8192,128]{1,0:T(8,128)}), f32[128,128]{1,0:T(8,128)}) %reduce-scatter.10.cloned.1.call-update) | async-done | bytes 65552 | tf_op jit(solution)/shard_map/reduce_scatter | solution.py:97
  (144 shorter events, 75.7 us)
Async XLA Ops:
  7.2 124.6 %copy-start = (bf16[512,128]{1,0:T(8,128)(2,1)S(1)}, bf16[512,128]{1,0:T(8,128)(2,1)}, u32[]{:S(2)}) copy-start(bf16[512,128]{1,0:T(8,128)(2,1)} %param.26) | copy-start | bytes 393220
  7.2 83.9 %all-gather.6.cloned.1.call-start = ((), (), s32[]{:S(2)}) async-start(), calls=%async_computation.4 | async-start | bytes 2129920 | tf_op jit(solution)/shard_map/all_gather | solution.py:68
  7.9 123.9 %all-gather.4.cloned.1.call-start = ((), (), s32[]{:S(2)}) async-start(), calls=%async_computation.3 | async-start | bytes 1310720 | tf_op jit(solution)/shard_map/all_gather | solution.py:67
  8.7 418.1 %reduce-scatter.6.cloned.1.call-start = ((), (), s32[]{:S(2)}) async-start(), calls=%async_computation.5 | async-start | bytes 4259840 | tf_op jit(solution)/shard_map/reduce_scatter | solution.py:71
  158.4 0.7 copy-start.6
  158.4 256.8 %copy-start.4 = (bf16[128,128]{1,0:T(8,128)(2,1)S(1)}, bf16[128,128]{1,0:T(8,128)(2,1)}, u32[]{:S(2)}) copy-start(bf16[128,128]{1,0:T(8,128)(2,1)} %param.25) | copy-start | bytes 98308
  158.4 268.1 %copy-start.2 = (bf16[512,128]{1,0:T(8,128)(2,1)S(1)}, bf16[512,128]{1,0:T(8,128)(2,1)}, u32[]{:S(2)}) copy-start(bf16[512,128]{1,0:T(8,128)(2,1)} %param.27) | copy-start | bytes 393220
  158.4 279.7 %copy-start.3 = (bf16[512,128]{1,0:T(8,128)(2,1)S(1)}, bf16[512,128]{1,0:T(8,128)(2,1)}, u32[]{:S(2)}) copy-start(bf16[512,128]{1,0:T(8,128)(2,1)} %param.28) | copy-start | bytes 393220
  158.5 279.7 %copy-start.5 = (bf16[128,128]{1,0:T(8,128)(2,1)S(1)}, bf16[128,128]{1,0:T(8,128)(2,1)}, u32[]{:S(2)}) copy-start(bf16[128,128]{1,0:T(8,128)(2,1)} %param.29) | copy-start | bytes 98308
  158.5 300.4 %reduce-scatter.8.cloned.1.call-start = ((), (), s32[]{:S(2)}) async-start(), calls=%async_computation.6 | async-start | bytes 327680 | tf_op jit(solution)/shard_map/reduce_scatter | solution.py:91
  439.9 101.0 %all-gather.8.cloned.1.call-start = ((), (), s32[]{:S(2)}) async-start(), calls=%async_computation.7 | async-start | bytes 2129920 | tf_op jit(solution)/shard_map/all_gather | solution.py:93
  460.4 304.3 %all-reduce.7.cloned.1.call-start = ((), (), s32[]{:S(2)}) async-start(), calls=%async_computation.9 | async-start | bytes 1572864
  540.9 40.9 %copy-start.1 = (bf16[1024,512]{1,0:T(8,128)(2,1)S(1)}, bf16[1024,512]{1,0:T(8,128)(2,1)}, u32[]{:S(2)}) copy-start(bf16[1024,512]{1,0:T(8,128)(2,1)} %all-gather.4.cloned.1.call-done) | copy-start | bytes 3145732
  582.9 329.8 %reduce-scatter.10.cloned.1.call-start = ((), (), s32[]{:S(2)}) async-start(), calls=%async_computation.8 | async-start | bytes 4259840 | tf_op jit(solution)/shard_map/reduce_scatter | solution.py:97
Sparse Core Ops, SparseCore 0:
  10.8 80.2 all-gather.5
  92.9 25.4 all-gather.3
  158.6 141.5 reduce-scatter.5
  440.0 18.7 reduce-scatter.7
  462.0 78.8 all-gather.7
  583.0 181.6 all-reduce.6
  770.0 142.6 reduce-scatter.9
where the time goes:
time: 921 us; the launch traced here: 920 us
  waiting for transfers between devices  479 us (52%)
  blocking collectives  271 us (29%)
  matrix products  61.8 us (7%)
  loops' own time  52.5 us (6%)
  local copies, waits for them, and re-layouts  28 us (3%)
  between operations  15.6 us (2%)
  other arithmetic  11.6 us (1%)
    unnamed x1, blocking collectives  249 us
    unnamed x8, waiting for transfers between devices  158 us
    reduce_scatter x1, waiting for transfers between devices, shards(): lax.psum_scatter(sum_rows(fact_dim, d_msgpre, dim_local * lax.axis_size('...  144 us
    all_gather x1, waiting for transfers between devices, shards(): lax.all_gather(dim_table, 'fact', axis=0, tiled=True)  79.6 us
    all_gather x1, waiting for transfers between devices, shards(): lax.all_gather(d_scaled, 'fact', axis=0, tiled=True)  78.6 us
    another operation x2, loops' own time, pick_rows(): lax.scan(advance, initial, jnp.arange(num_blocks, dtype=jnp.int32))  42 us
    dot_general x16, matrix products, advance(): jnp.dot(selector, block, preferred_element_type=jnp.float32)  30 us
    dot_general x16, matrix products, column_block(): return jnp.dot(selector, values, preferred_element_type=jnp.float32)  25.3 us
  transfers between devices with their start and end apart: 7, of which 5 were waited for; matrix products, arithmetic and copies ran while one was open for 6% of the time, Pallas kernels for 0%

commit v1 on v0

--- a/solution.py
+++ b/solution.py
@@ -90,9 +90,12 @@
     agg_term = jnp.einsum("ej,aj->ea", d_pre, w_neigh, preferred_element_type=jnp.float32)
     d_agg = lax.psum_scatter(agg_term, "feat", scatter_dimension=1, tiled=True)
     d_scaled = (d_agg / divisor[:, None]).astype(jnp.bfloat16)
-    d_message = pick_rows(entity, lax.all_gather(d_scaled, "fact", axis=0, tiled=True)).astype(
-        jnp.bfloat16
-    )
+    d_message = pick_rows(
+        entity,
+        jnp.concatenate(
+            lax.all_to_all(jnp.stack([d_scaled] * lax.axis_size("fact")), "fact", 0, 0), axis=0
+        ),
+    ).astype(jnp.bfloat16)
     d_msgpre = (d_message.astype(jnp.float32) * silu_slope(msg_pre)).astype(jnp.bfloat16)
     grad_dim = lax.psum_scatter(
         sum_rows(fact_dim, d_msgpre, dim_local * lax.axis_size("fact")),

time: 921 us -> 910 us (0.988)
  waiting for transfers between devices: 479 us -> 449 us
  starting transfers between devices: 0.28 us -> 10.7 us
    all_gather x1 -> x0, waiting for transfers between devices: 78.6 us -> none  [shards(): lax.all_gather(d_scaled, 'fact', axis=0, tiled=True)]
    all_to_all x0 -> x1, waiting for transfers between devices: none -> 49.5 us  [shards(): lax.all_to_all(jnp.stack([d_scaled] * lax.axis_size('fact')), 'fact', 0, 0)]
    all_to_all x0 -> x1, starting transfers between devices: none -> 10.5 us  [shards(): lax.all_to_all(jnp.stack([d_scaled] * lax.axis_size('fact')), 'fact', 0, 0)]
    unnamed x8 -> x7, waiting for transfers between devices: 158 us -> 156 us
where the time goes in v1:
time: 910 us; the launch traced here: 908 us
  waiting for transfers between devices  449 us (49%)
  blocking collectives  271 us (30%)
  matrix products  67.9 us (7%)
  loops' own time  52.4 us (6%)
  local copies, waits for them, and re-layouts  29.9 us (3%)
  between operations  15.6 us (2%)
  other arithmetic  12.2 us (1%)
  starting transfers between devices  10.7 us (1%)
    unnamed x1, blocking collectives  249 us
    unnamed x7, waiting for transfers between devices  156 us
    reduce_scatter x1, waiting for transfers between devices, shards(): lax.psum_scatter(sum_rows(fact_dim, d_msgpre, dim_local * lax.axis_size('...  144 us
    all_gather x1, waiting for transfers between devices, shards(): lax.all_gather(dim_table, 'fact', axis=0, tiled=True)  79.6 us
    all_to_all x1, waiting for transfers between devices, shards(): lax.all_to_all(jnp.stack([d_scaled] * lax.axis_size('fact')), 'fact', 0, 0)  49.5 us
    another operation x2, loops' own time, pick_rows(): lax.scan(advance, initial, jnp.arange(num_blocks, dtype=jnp.int32))  41.8 us
    dot_general x16, matrix products, advance(): jnp.dot(selector, block, preferred_element_type=jnp.float32)  35.3 us
    dot_general x16, matrix products, column_block(): return jnp.dot(selector, values, preferred_element_type=jnp.float32)  25.4 us
  transfers between devices with their start and end apart: 7, of which 5 were waited for; matrix products, arithmetic and copies ran while one was open for 6% of the time, Pallas kernels for 0%

profile of v1, /device:TPU:2, one launch (start us, length us, event | category | flops | bytes accessed | tf_op | source)
XLA Modules:
  0.0 907.8 jit_solution(1403976932214309614)
XLA Ops:
  11.5 79.6 %all-gather.5.cloned.1.call-done = bf16[8192,128]{1,0:T(8,128)(2,1)} async-done(((bf16[128,128]{1,0:T(8,128)(2,1)}), bf16[8192,128]{1,0:T(8,128)(2,1)}) %all-gather.5.cloned.1.call-update) | async-done | bytes 2097168 | tf_op jit(solution)/shard_map/all_gather | solution.py:68
  91.1 40.7 %while.46 = (s32[]{:T(128)}, f32[1024,128]{1,0:T(8,128)S(1)}, s32[1024]{0:T(1024)S(1)}, s32[8]{0:T(128)S(1)}, bf16[8,1024,128]{2,1,0:T(8,128)(2,1)}, /*index=5*/s32[]{:T(128)}, s32[]{:T(128)}, s32[]{:T(128)}, s32[]{:T(128)}) while((s32[]{:T(128)}, f32[1024,128]{1,0:T(8,128)S(1)}, s32[1024]{0:T(1024)S(1)}, s32[8]{0:T(128)S(1)}, ...), condition=%wide.region_1.2_spmd.clone, body=%wide.region_0.1_spmd.clone.sunk | while | flops 269747200 | bytes 1323177 | solution.py:28
  131.8 2.5 multiply_convert_fusion.1
  134.3 2.3 broadcast.45.clone
  136.6 22.7 %while.44 = (s32[]{:T(128)}, f32[8,1024,128]{2,1,0:T(8,128)}, s32[8]{0:T(128)S(1)}, s32[1024]{0:T(1024)S(1)}, bf16[1024,128]{1,0:T(8,128)(2,1)S(1)}, /*index=5*/s32[]{:T(128)}, s32[1]{0:T(128)}) while((s32[]{:T(128)}, f32[8,1024,128]{2,1,0:T(8,128)}, s32[8]{0:T(128)S(1)}, s32[1024]{0:T(1024)S(1)}, bf16[1024,128]{1,0:T(8,128)(2,1)S(1)}, ...), condition=%wide.region_3.4_spmd.clone, body=%wide.region_2.3_spmd.clone.sunk | while | flops 269485056 | bytes 799337 | solution.py:43
  161.2 5.9 scatter_custom_fusion
  167.2 248.8 %all-reduce = f32[8192]{0:T(1024)S(1)} all-reduce(f32[8192]{0:T(1024)S(1)} %scatter_custom_fusion), channel_id=3, replica_groups=mesh['fact'=64,'feat'=4] {'fact'}, use_global_device_ids=true, to_apply=%region_6.7.clone | all-reduce | flops 8192 | bytes 65536
  416.0 11.4 %all_gather.12 = bf16[128,512]{1,0:T(8,128)(2,1)S(1)} all-gather(bf16[128,128]{1,0:T(8,128)(2,1)S(1)} %copy-done.4), channel_id=1, replica_groups=mesh['fact'=64,'feat'=4] {'feat'}, dimensions={1}, use_global_device_ids=true | all-gather | bytes 163840 | tf_op jit(solution)/shard_map/all_gather | solution.py:82
  428.6 10.4 %all_gather.15 = bf16[128,512]{1,0:T(8,128)(2,1)S(1)} all-gather(bf16[128,128]{1,0:T(8,128)(2,1)S(1)} %divide_convert_fusion.1), channel_id=1, replica_groups=mesh['fact'=64,'feat'=4] {'feat'}, dimensions={1}, use_global_device_ids=true | all-gather | bytes 163840 | tf_op jit(solution)/shard_map/all_gather | solution.py:83
  440.7 18.9 %reduce-scatter.8.cloned.1.call-done = f32[128,128]{1,0:T(8,128)} async-done(((f32[128,512]{1,0:T(8,128)}), f32[128,128]{1,0:T(8,128)}) %reduce-scatter.8.cloned.1.call-update) | async-done | bytes 65552 | tf_op jit(solution)/shard_map/reduce_scatter | solution.py:91
  462.4 10.5 %all-to-all-start = ((bf16[64,128,128]{2,1,0:T(8,128)(2,1)}), bf16[64,128,128]{2,1,0:T(8,128)(2,1)S(1)}, u32[]{:S(2)}, u32[]{:S(2)}) async-start(bf16[64,128,128]{2,1,0:T(8,128)(2,1)} %stack.2), calls=%async_computation.2 | async-start | bytes 4194304 | tf_op jit(solution)/shard_map/all_to_all | solution.py:96
  474.8 49.5 %all-to-all-done = bf16[64,128,128]{2,1,0:T(8,128)(2,1)S(1)} async-done(((bf16[64,128,128]{2,1,0:T(8,128)(2,1)}), bf16[64,128,128]{2,1,0:T(8,128)(2,1)S(1)}, u32[]{:S(2)}, u32[]{:S(2)}) %all-to-all-start) | async-done | bytes 2097184 | tf_op jit(solution)/shard_map/all_to_all | solution.py:96
  524.2 45.8 %while.47 = (s32[]{:T(128)}, f32[1024,128]{1,0:T(8,128)}, s32[1024]{0:T(1024)S(1)}, s32[8]{0:T(128)S(1)}, bf16[8,1024,128]{2,1,0:T(8,128)(2,1)S(1)}, /*index=5*/s32[]{:T(128)}, s32[]{:T(128)}, s32[]{:T(128)}, s32[]{:T(128)}) while((s32[]{:T(128)}, f32[1024,128]{1,0:T(8,128)}, s32[1024]{0:T(1024)S(1)}, s32[8]{0:T(128)S(1)}, ...), condition=%wide.region_9.10_spmd.clone, body=%wide.region_8.9_spmd.clone.sunk | while | flops 269747200 | bytes 1323177 | solution.py:28
  532.2 2.7 fusion.76
  538.1 2.7 fusion.76
  543.9 2.7 fusion.76
  549.8 2.7 fusion.76
  555.6 2.7 fusion.76
  561.5 2.7 fusion.76
  567.4 2.7 fusion.76
  572.5 2.3 broadcast.45
  574.8 22.7 %while.45 = (s32[]{:T(128)}, f32[8,1024,128]{2,1,0:T(8,128)}, s32[8]{0:T(128)S(1)}, s32[1024]{0:T(1024)S(1)}, bf16[1024,128]{1,0:T(8,128)(2,1)S(1)}, /*index=5*/s32[]{:T(128)}, s32[1]{0:T(128)}) while((s32[]{:T(128)}, f32[8,1024,128]{2,1,0:T(8,128)}, s32[8]{0:T(128)S(1)}, s32[1024]{0:T(1024)S(1)}, ...), condition=%wide.region_14.15_spmd.clone, body=%wide.region_13.14_spmd.clone.sunk | while | flops 269485056 | bytes 799337 | solution.py:43
  598.2 155.0 %all-reduce.7.cloned.1.call-done = (f32[512,128]{0,1:T(8,128)}, f32[512,128]{0,1:T(8,128)}, f32[512,128]{1,0:T(8,128)}) async-done(((f32[512,128]{0,1:T(8,128)}, f32[512,128]{0,1:T(8,128)}, f32[512,128]{1,0:T(8,128)}), (f32[512,128]{0,1:T(8,128)}, f32[512,128]{0,1:T(8,128)}, f32[512,128]{1,0:T(8,128)})) %all-reduce.7.cloned.1.call-update) | async-done | bytes 786448
  756.7 144.2 %reduce-scatter.10.cloned.1.call-done = f32[128,128]{1,0:T(8,128)} async-done(((f32[8192,128]{1,0:T(8,128)}), f32[128,128]{1,0:T(8,128)}) %reduce-scatter.10.cloned.1.call-update) | async-done | bytes 65552 | tf_op jit(solution)/shard_map/reduce_scatter | solution.py:100
  (144 shorter events, 80.0 us)
Async XLA Ops:
  7.2 124.6 %copy-start = (bf16[512,128]{1,0:T(8,128)(2,1)S(1)}, bf16[512,128]{1,0:T(8,128)(2,1)}, u32[]{:S(2)}) copy-start(bf16[512,128]{1,0:T(8,128)(2,1)} %param.26) | copy-start | bytes 393220
  7.2 83.9 %all-gather.5.cloned.1.call-start = ((), (), s32[]{:S(2)}) async-start(), calls=%async_computation.5 | async-start | bytes 2129920 | tf_op jit(solution)/shard_map/all_gather | solution.py:68
  7.9 123.9 %all-gather.3.cloned.1.call-start = ((), (), s32[]{:S(2)}) async-start(), calls=%async_computation.4 | async-start | bytes 1310720 | tf_op jit(solution)/shard_map/all_gather | solution.py:67
  8.7 419.0 %reduce-scatter.6.cloned.1.call-start = ((), (), s32[]{:S(2)}) async-start(), calls=%async_computation.6 | async-start | bytes 4259840 | tf_op jit(solution)/shard_map/reduce_scatter | solution.py:71
  159.3 0.7 copy-start.6
  159.3 256.7 %copy-start.4 = (bf16[128,128]{1,0:T(8,128)(2,1)S(1)}, bf16[128,128]{1,0:T(8,128)(2,1)}, u32[]{:S(2)}) copy-start(bf16[128,128]{1,0:T(8,128)(2,1)} %param.25) | copy-start | bytes 98308
  159.3 268.1 %copy-start.2 = (bf16[512,128]{1,0:T(8,128)(2,1)S(1)}, bf16[512,128]{1,0:T(8,128)(2,1)}, u32[]{:S(2)}) copy-start(bf16[512,128]{1,0:T(8,128)(2,1)} %param.27) | copy-start | bytes 393220
  159.3 279.7 %copy-start.3 = (bf16[512,128]{1,0:T(8,128)(2,1)S(1)}, bf16[512,128]{1,0:T(8,128)(2,1)}, u32[]{:S(2)}) copy-start(bf16[512,128]{1,0:T(8,128)(2,1)} %param.28) | copy-start | bytes 393220
  159.3 279.7 %copy-start.5 = (bf16[128,128]{1,0:T(8,128)(2,1)S(1)}, bf16[128,128]{1,0:T(8,128)(2,1)}, u32[]{:S(2)}) copy-start(bf16[128,128]{1,0:T(8,128)(2,1)} %param.29) | copy-start | bytes 98308
  159.3 300.3 %reduce-scatter.8.cloned.1.call-start = ((), (), s32[]{:S(2)}) async-start(), calls=%async_computation.7 | async-start | bytes 327680 | tf_op jit(solution)/shard_map/reduce_scatter | solution.py:91
  462.4 61.8 %all-to-all-start = ((bf16[64,128,128]{2,1,0:T(8,128)(2,1)}), bf16[64,128,128]{2,1,0:T(8,128)(2,1)S(1)}, u32[]{:S(2)}, u32[]{:S(2)}) async-start(bf16[64,128,128]{2,1,0:T(8,128)(2,1)} %stack.2), calls=%async_computation.2 | async-start | bytes 4194304 | tf_op jit(solution)/shard_map/all_to_all | solution.py:96
  472.9 280.3 %all-reduce.7.cloned.1.call-start = ((), (), s32[]{:S(2)}) async-start(), calls=%async_computation.9 | async-start | bytes 1572864
  524.2 47.2 %copy-start.1 = (bf16[1024,512]{1,0:T(8,128)(2,1)S(1)}, bf16[1024,512]{1,0:T(8,128)(2,1)}, u32[]{:S(2)}) copy-start(bf16[1024,512]{1,0:T(8,128)(2,1)} %all-gather.3.cloned.1.call-done) | copy-start | bytes 3145732
  572.5 328.5 %reduce-scatter.10.cloned.1.call-start = ((), (), s32[]{:S(2)}) async-start(), calls=%async_computation.8 | async-start | bytes 4259840 | tf_op jit(solution)/shard_map/reduce_scatter | solution.py:100
Sparse Core Ops, SparseCore 0:
  10.8 80.2 all-gather.4
  92.9 25.4 all-gather.2
  159.4 141.6 reduce-scatter.5
  440.9 18.7 reduce-scatter.7
  572.6 180.5 all-reduce.6
  758.3 142.6 reduce-scatter.9
